TPU v7x, 32 devices: a whole 2x2x4 slice. The times are simulated.
32 devices in a mesh: feed: 8 (over y, x, core), tm: 4 (over z).
Axes of the slice: x: 2, y: 2, z: 4, core: 2. Of those that a mesh axis runs over, the one named last changes fastest.
Arguments:
- voltages: bfloat16 [256, 1048576], P('feed', 'tm'), may hold values from -12 to 12
- filter_taps: float32 [4, 1024], replicated, may hold values from -1 to 1
- delays: float32 [256], P('feed'), may hold values from -64 to 64
- channel_flags: int32 [512], P('feed'), may hold values from 0 to 1, as said below
Outputs:
- visibilities: float32 [512, 256, 256], P(('feed', 'tm'))
Inputs may be any that keep to these rules, and one draw needn't show every extreme that they name: `channel_flags`: channel c belongs to owner c // 64; every owner keeps between 16 and 64 of its channels, and in every draw some owner keeps all of them.
All inputs are finite; a program needn't handle non-finite values.
Results may differ from a plain program's by a relative error of at most 0.0011.
Values may be sent and summed in bfloat16 or wider, within the bound.
A program may use at most 192 MiB of HBM per device.

v0:
```python
import math
import jax
import jax.numpy as jnp
from jax import lax
from jax.sharding import PartitionSpec as P


def passed_along(block, axis, distance):
    devices = range(lax.axis_size(axis))
    route = [(i - distance, i) for i in devices if i - distance in devices]
    return lax.ppermute(block, axis, route)


def build_table(fft_length):
    channels = jnp.arange(fft_length // 2, dtype=jnp.int32)
    samples = jnp.arange(fft_length, dtype=jnp.int32)
    product = channels[:, None] * samples[None, :] % fft_length
    angles = product.astype(jnp.float32) * (2.0 * math.pi / fft_length)
    return jnp.stack([jnp.cos(angles), -jnp.sin(angles)], axis=1).astype(jnp.bfloat16)


def rotate_phase(real_part, imag_part, channels, delay_values, fft_length):
    angles = 2.0 * math.pi / fft_length * channels * delay_values
    cosine = jnp.cos(angles)
    sine_part = jnp.sin(angles)
    factor = 1.0 / math.sqrt(fft_length)
    return (
        (real_part * cosine + imag_part * sine_part) * factor,
        (imag_part * cosine - real_part * sine_part) * factor,
    )


def gram_blocks(turned, local_frame_count, frame_total):
    count_here, inputs_all, columns = turned.shape
    split = turned.reshape(
        count_here, inputs_all, columns // (2 * local_frame_count), 2, local_frame_count
    )
    real_half = split[:, :, :, 0].reshape(count_here, inputs_all, columns // 2)
    imag_half = split[:, :, :, 1].reshape(count_here, inputs_all, columns // 2)
    block_rows = min(128, inputs_all)
    column_index = jnp.arange(inputs_all)[None, :]
    row_blocks = []
    for first in range(0, inputs_all, block_rows):
        last = first + block_rows
        upper = jnp.einsum(
            "cik,cjk->cij",
            turned[:, first:last],
            turned[:, first:],
            preferred_element_type=jnp.float32,
        )
        lower = jnp.einsum(
            "cik,cjk->cij",
            imag_half[:, first:last],
            real_half[:, :last],
            preferred_element_type=jnp.float32,
        )
        lower = lower - jnp.einsum(
            "cik,cjk->cij",
            real_half[:, first:last],
            imag_half[:, :last],
            preferred_element_type=jnp.float32,
        )
        upper_full = jnp.pad(upper, ((0, 0), (0, 0), (first, 0)))
        lower_full = jnp.pad(lower, ((0, 0), (0, 0), (0, inputs_all - last)))
        row_index = jnp.arange(first, last)[:, None]
        row_blocks.append(jnp.where(row_index <= column_index, upper_full, lower_full))
    return jnp.concatenate(row_blocks, axis=1) / frame_total


def on_device(voltages, filter_taps, delays, channel_flags):
    inputs_here, sample_count = voltages.shape
    tap_count, fft_length = filter_taps.shape
    local_frame_count = sample_count // fft_length
    frames = voltages.reshape(inputs_here, local_frame_count, fft_length)
    history = passed_along(frames[:, local_frame_count - (tap_count - 1) :, :], "tm", 1)
    extended = jnp.concatenate([history, frames], axis=1).astype(jnp.float32)
    filtered = filter_taps[0] * extended[:, tap_count - 1 : tap_count - 1 + local_frame_count]
    for tap_index in range(1, tap_count):
        offset = tap_count - 1 - tap_index
        filtered = (
            filtered + filter_taps[tap_index] * extended[:, offset : offset + local_frame_count]
        )
    filtered = filtered.astype(jnp.bfloat16)
    dft_table = build_table(fft_length)
    raw_spectra = jnp.einsum(
        "cpn,isn->cips", dft_table, filtered, preferred_element_type=jnp.float32
    )
    channels = jnp.arange(fft_length // 2).astype(jnp.float32)[:, None, None]
    real_part, imag_part = rotate_phase(
        raw_spectra[:, :, 0], raw_spectra[:, :, 1], channels, delays[None, :, None], fft_length
    )
    spectra = jnp.concatenate([real_part, imag_part], axis=2).astype(jnp.bfloat16)
    time_devices = lax.axis_size("tm")
    frame_total = local_frame_count * time_devices
    channels_here = channel_flags.shape[0] // time_devices
    local_flags = lax.dynamic_slice_in_dim(
        channel_flags, lax.axis_index("tm") * channels_here, channels_here, 0
    )
    turned = lax.all_to_all(spectra, "feed", split_axis=0, concat_axis=1, tiled=True)
    visibility = lax.psum_scatter(
        gram_blocks(turned, local_frame_count, frame_total), "tm", scatter_dimension=0, tiled=True
    )
    return visibility * local_flags[:, None, None].astype(jnp.float32)


def solution(mesh):
    in_specs = (P("feed", "tm"), P(), P("feed"), P("feed"))
    out_specs = P(("feed", "tm"), None, None)
    return jax.shard_map(
        on_device, mesh=mesh, in_specs=in_specs, out_specs=out_specs, check_vma=False
    )
```

profile of v0, /device:TPU:0, one launch (start us, length us, event | category | flops | bytes accessed | tf_op | source)
XLA Modules:
  0.0 797.1 jit_solution(467650899731393742)
XLA Ops:
  6.5 15.4 %copy.23 = bf16[4,8,256,1024]{3,2,1,0:T(8,128)(2,1)S(1)} copy(bf16[4,8,256,1024]{3,1,2,0:T(8,128)(2,1)} %bitcast.67) | data formatting | bytes 33554432
  21.9 0.1 slice.79
  22.1 4.9 collective-permute-start
  27.0 8.5 %negate_convert_fusion = (bf16[512,1,1024]{2,0,1:T(8,128)(2,1)S(1)}, bf16[512,1,1024]{2,0,1:T(8,128)(2,1)S(1)}) fusion(), kind=kLoop, calls=%fused_computation.49 | loop fusion | flops 8912896 | bytes 2097152 | tf_op jit(solution)/shard_map/convert.3
  35.6 0.3 multiply_cosine_fusion
  35.9 12.0 %maximum_convert_fusion = f32[32,259,1024]{2,1,0:T(8,128)} fusion(bf16[32,256,1024]{2,1,0:T(8,128)(2,1)S(1)} %bitcast.66, bf16[32,3,1024]{2,1,0:T(4,128)(2,1)S(1)} %collective-permute-done), kind=kLoop, calls=%fused_computation.8 | loop fusion | flops 33947648 | bytes 50921472 | tf_op jit(solution)/shard_map/convert_element_type | solution.py:76
  47.9 56.9 %fusion.10 = f32[512,32,2,256]{0,3,2,1:T(8,128)} fusion(f32[32,259,1024]{2,1,0:T(8,128)} %maximum_convert_fusion, f32[1024]{0:T(1024)S(1)} %bitcast.70, f32[1024]{0:T(1024)S(1)} %bitcast.71, f32[1024]{0:T(1024)S(1)} %bitcast.69, f32[1024]{0:T(1024)S(1)} %bitcast.68, bf16[512,1,1024]{2,0,1:T(8,128)(2,1)S(1)} %get-tuple-element.15, ...), kind=kOutput, calls=%fused_computation.20 | convolution fusion | flops 17251172352 | bytes 169885696 | tf_op jit(solution)/shard_map/cpn,isn->cips/dot_general | solution.py:85
  104.8 12.3 %multiply_convert_fusion.1 = (bf16[512,32,256]{0,2,1:T(8,128)(2,1)S(1)}, bf16[512,32,256]{0,2,1:T(8,128)(2,1)S(1)}) fusion(f32[512,32,2,256]{0,3,2,1:T(8,128)} %fusion.10, f32[512,32]{0,1:T(8,128)S(1)} %get-tuple-element.14, f32[512,32]{0,1:T(8,128)S(1)} %get-tuple-element.13), kind=kLoop, calls=%fused_computation.16 | loop fusion | flops 41943040 | bytes 50462720 | tf_op jit(solution)/shard_map/convert
  117.1 6.5 pad_maximum_fusion
  123.6 28.6 %copy.14 = bf16[512,32,512]{2,1,0:T(8,128)(2,1)} copy(bf16[512,32,512]{0,2,1:T(8,128)(2,1)} %pad_maximum_fusion) | data formatting | bytes 33554432 | tf_op jit(solution)/shard_map/concatenate | solution.py:92
  152.3 5.7 all-to-all-start
  158.0 0.2 reduce-scatter.2.cloned.1.call-start
  158.3 0.1 iota_compare_fusion
  158.4 183.6 %all-to-all-done = bf16[512,32,512]{2,1,0:T(8,128)(2,1)} async-done(((bf16[512,32,512]{2,1,0:T(8,128)(2,1)}), bf16[512,32,512]{2,1,0:T(8,128)(2,1)}, u32[]{:S(2)}, u32[]{:S(2)}) %all-to-all-start) | async-done | bytes 16777248 | tf_op jit(solution)/shard_map/all_to_all | solution.py:99
  341.9 14.1 %copy.15 = bf16[64,8,32,512]{3,2,1,0:T(8,128)(2,1)} copy(bf16[64,8,32,512]{3,2,0,1:T(8,128)(2,1)} %bitcast.11) | data formatting | bytes 33554432 | tf_op jit(solution)/shard_map/all_to_all | solution.py:99
  356.0 23.7 %reshape.151 = bf16[64,256,1,2,256]{4,3,1,0,2:T(2,128)(2,1)} reshape(bf16[64,8,32,512]{3,2,1,0:T(8,128)(2,1)} %copy.15) | data formatting | bytes 33554432 | tf_op jit(solution)/shard_map/reshape | solution.py:35
  379.7 32.4 %fusion.45 = (bf16[64,256,1,1,256]{4,3,1,0,2:T(2,128)(2,1)}, bf16[64,256,1,1,256]{4,3,1,0,2:T(2,128)(2,1)}) fusion(bf16[64,256,1,2,256]{4,3,1,0,2:T(2,128)(2,1)} %reshape.151), kind=kLoop, calls=%fused_computation.63 | loop fusion | bytes 33554432 | tf_op jit(solution)/shard_map/slice | solution.py:38
  412.2 8.9 %copy.26 = bf16[64,256,1,1,256]{4,1,0,3,2:T(8,128)(2,1)S(1)} copy(bf16[64,256,1,1,256]{4,3,1,0,2:T(2,128)(2,1)} %get-tuple-element.7) | data formatting | bytes 16777216
  421.1 11.9 %copy.27 = bf16[64,256,1,1,256]{4,1,0,3,2:T(8,128)(2,1)S(1)} copy(bf16[64,256,1,1,256]{4,3,1,0,2:T(2,128)(2,1)} %get-tuple-element.8) | data formatting | bytes 16777216
  433.1 3.2 copy-done.1
  436.3 3.3 fusion.21
  439.6 9.5 %fusion.17 = f32[64,128,256]{2,1,0:T(8,128)} fusion(bf16[64,256,256]{2,1,0:T(8,128)(2,1)} %bitcast.62, bf16[64,256,256]{2,1,0:T(8,128)(2,1)S(1)} %bitcast.58), kind=kOutput, calls=%fused_computation.29 | convolution fusion | flops 1073741824 | bytes 20971520 | tf_op jit(solution)/shard_map/cik,cjk->cij/dot_general | solution.py:57
  449.0 6.8 fusion.37
  455.9 10.1 %fusion.13 = f32[64,128,128]{2,1,0:T(8,128)} fusion(bf16[64,256,512]{2,1,0:T(8,128)(2,1)} %bitcast.55), kind=kOutput, calls=%fused_computation.21 | convolution fusion | flops 1073741824 | bytes 12582912 | tf_op jit(solution)/shard_map/cik,cjk->cij/dot_general | solution.py:45
  466.0 15.0 %pad_select_fusion = f32[64,128,256]{2,1,0:T(8,128)} fusion(f32[64,128,128]{2,1,0:T(8,128)} %fusion.37, pred[128,256]{1,0:T(8,128)(4,1)S(1)} %iota_compare_fusion.1, bf16[64,256,512]{2,1,0:T(8,128)(2,1)} %bitcast.56), kind=kOutput, calls=%fused_computation.28 | convolution fusion | flops 2149580800 | bytes 37781504 | tf_op jit(solution)/shard_map/cik,cjk->cij/dot_general | solution.py:45
  481.0 14.2 %subtract_select_fusion = f32[64,128,256]{2,1,0:T(8,128)} fusion(f32[64,128,256]{2,1,0:T(8,128)} %fusion.17, f32[64,128,128]{2,1,0:T(8,128)} %fusion.13, pred[128,256]{1,0:T(8,128)(4,1)S(1)} %iota_compare_fusion, bf16[64,256,256]{2,1,0:T(8,128)(2,1)} %bitcast.60, bf16[64,256,256]{2,1,0:T(8,128)(2,1)} %bitcast.64), kind=kOutput, calls=%fused_computation.27 | convolution fusion | flops 1077936128 | bytes 33587200 | tf_op jit(solution)/shard_map/cik,cjk->cij/dot_general | solution.py:51
  495.2 11.4 %maximum_multiply_fusion = f32[64,256,256]{2,1,0:T(8,128)} fusion(f32[64,128,256]{2,1,0:T(8,128)} %subtract_select_fusion, f32[64,128,256]{2,1,0:T(8,128)} %pad_select_fusion), kind=kLoop, calls=%fused_computation.12 | loop fusion | flops 8388608 | bytes 33554432 | tf_op jit(solution)/shard_map/div | solution.py:67
  506.7 0.0 reduce-scatter.2.cloned.1.call-update
  506.7 0.6 copy-done.4
  507.3 0.1 dynamic-slice_convert_fusion
  507.4 278.1 %reduce-scatter.2.cloned.1.call-done = f32[16,256,256]{2,1,0:T(8,128)} async-done(((f32[64,256,256]{2,1,0:T(8,128)}), f32[16,256,256]{2,1,0:T(8,128)}) %reduce-scatter.2.cloned.1.call-update) | async-done | bytes 4194320 | tf_op jit(solution)/shard_map/reduce_scatter | solution.py:100
  785.5 4.7 broadcast_multiply_fusion
  (13 shorter events, 0.1 us)
Async XLA Ops:
  6.5 29.0 %copy-start.3 = (f32[32]{0:T(128)S(1)}, f32[32]{0:T(128)}, u32[]{:S(2)}) copy-start(f32[32]{0:T(128)} %param.6) | copy-start | bytes 388
  6.5 29.3 %copy-start.2 = (f32[4,1024]{1,0:T(4,128)S(1)}, f32[4,1024]{1,0:T(4,128)}, u32[]{:S(2)}) copy-start(f32[4,1024]{1,0:T(4,128)} %param.5) | copy-start | bytes 49156
  22.1 13.8 %collective-permute-start = (bf16[32,3,1024]{2,1,0:T(4,128)(2,1)S(1)}, bf16[32,3,1024]{2,1,0:T(4,128)(2,1)S(1)}, u32[]{:S(2)}, u32[]{:S(2)}) collective-permute-start(bf16[32,3,1024]{2,1,0:T(4,128)(2,1)S(1)} %slice.79), channel_id=1, source_target_pairs={{0,1},{1,2},{2,3},{4,5},{5,6},{6,7},{8,9},{9,10},{10,11},{12,13},{... | collective-permute-start | bytes 589832 | tf_op jit(solution)/shard_map/ppermute | solution.py:11
  152.3 189.7 %all-to-all-start = ((bf16[512,32,512]{2,1,0:T(8,128)(2,1)}), bf16[512,32,512]{2,1,0:T(8,128)(2,1)}, u32[]{:S(2)}, u32[]{:S(2)}) async-start(bf16[512,32,512]{2,1,0:T(8,128)(2,1)} %copy.14), calls=%async_computation | async-start | bytes 33554432 | tf_op jit(solution)/shard_map/all_to_all | solution.py:99
  158.0 627.5 %reduce-scatter.2.cloned.1.call-start = ((), (), s32[]{:S(2)}) async-start(), calls=%async_computation.2 | async-start | bytes 20971520 | tf_op jit(solution)/shard_map/reduce_scatter | solution.py:100
  421.1 28.0 %copy-start = (bf16[64,256,1,1,256]{4,1,0,3,2:T(8,128)(2,1)}, bf16[64,256,1,1,256]{4,1,0,3,2:T(8,128)(2,1)S(1)}, u32[]{:S(2)}) copy-start(bf16[64,256,1,1,256]{4,1,0,3,2:T(8,128)(2,1)S(1)} %copy.26) | copy-start | bytes 25165828
  433.1 3.2 copy-start.1
  506.7 0.7 copy-start.4
Sparse Core Ops, SparseCore 0:
  506.8 278.6 reduce-scatter.1
where the time goes:
time: 799 us; the launch traced here: 797 us
  waiting for transfers between devices  462 us (58%)
  local copies, waits for them, and re-layouts  139 us (17%)
  matrix products  116 us (15%)
  other arithmetic  55.9 us (7%)
  between operations  13.6 us (2%)
  starting transfers between devices  10.9 us (1%)
    reduce_scatter x1, waiting for transfers between devices, on_device(): lax.psum_scatter(gram_blocks(turned, local_frame_count, frame_total), 'tm...  278 us
    all_to_all x1, waiting for transfers between devices, on_device(): lax.all_to_all(spectra, 'feed', split_axis=0, concat_axis=1, tiled=True)  184 us
    dot_general x1, matrix products, on_device(): jnp.einsum('cpn,isn->cips', dft_table, filtered, preferred_element_type=j...  56.9 us
    unnamed x13, local copies, waits for them, and re-layouts  40.1 us
    slice x1, local copies, waits for them, and re-layouts, gram_blocks(): real_half = split[:, :, :, 0].reshape(count_here, inputs_all, columns // 2)  32.4 us
    concatenate x1, local copies, waits for them, and re-layouts, on_device(): jnp.concatenate([real_part, imag_part], axis=2).astype(jnp.bfloat16)  28.6 us
    dot_general x2, matrix products, gram_blocks(): jnp.einsum('cik,cjk->cij', turned[:, first:last], turned[:, first:], pref...  25.1 us
    reshape x1, local copies, waits for them, and re-layouts, gram_blocks(): turned.reshape(count_here, inputs_all, columns // (2 * local_frame_count)...  23.7 us
  transfers between devices with their start and end apart: 3, of which 2 were waited for; matrix products, arithmetic and copies ran while one was open for 1% of the time, Pallas kernels for 0%

commit v1 on v0

--- a/solution.py
+++ b/solution.py
@@ -3,6 +3,12 @@
 import jax.numpy as jnp
 from jax import lax
 from jax.sharding import PartitionSpec as P
+
+
+def trade_parts(x, axis, split, join):
+    pieces = jnp.split(x, lax.axis_size(axis), axis=split)
+    got = lax.all_to_all(jnp.stack(pieces), axis, 0, 0)
+    return jnp.concatenate(got, axis=join)
 
 
 def passed_along(block, axis, distance):
@@ -96,7 +102,7 @@
     local_flags = lax.dynamic_slice_in_dim(
         channel_flags, lax.axis_index("tm") * channels_here, channels_here, 0
     )
-    turned = lax.all_to_all(spectra, "feed", split_axis=0, concat_axis=1, tiled=True)
+    turned = trade_parts(spectra, "feed", 0, 1)
     visibility = lax.psum_scatter(
         gram_blocks(turned, local_frame_count, frame_total), "tm", scatter_dimension=0, tiled=True
     )

time: 799 us -> 823 us (1.030)
  other arithmetic: 55.9 us -> 71.6 us
    another operation x0 -> x2, local copies, waits for them, and re-layouts: none -> 60.2 us  [the longest x1 36.5 us: trade_parts(): got = lax.all_to_all(jnp.stack(pieces), axis, 0, 0)]
    concatenate x1 -> x0, local copies, waits for them, and re-layouts: 28.6 us -> none  [on_device(): jnp.concatenate([real_part, imag_part], axis=2).astype(jnp.bfloat16)]
    unnamed x0 -> x7, other arithmetic: none -> 19 us
    all_to_all x1 -> x0, local copies, waits for them, and re-layouts: 14.1 us -> none  [on_device(): lax.all_to_all(spectra, 'feed', split_axis=0, concat_axis=1, tiled=True)]
    reshape x1, local copies, waits for them, and re-layouts: 23.7 us -> 14.1 us  [trade_parts(): return jnp.concatenate(got, axis=join)]
    another operation x2 -> x3, other arithmetic: 20.8 us -> 24 us
where the time goes in v1:
time: 823 us; the launch traced here: 821 us
  waiting for transfers between devices  462 us (56%)
  local copies, waits for them, and re-layouts  147 us (18%)
  matrix products  116 us (14%)
  other arithmetic  71.6 us (9%)
  between operations  13.6 us (2%)
  starting transfers between devices  10.7 us (1%)
    reduce_scatter x1, waiting for transfers between devices, on_device(): lax.psum_scatter(gram_blocks(turned, local_frame_count, frame_total), 'tm...  278 us
    all_to_all x1, waiting for transfers between devices, trade_parts(): got = lax.all_to_all(jnp.stack(pieces), axis, 0, 0)  184 us
    dot_general x1, matrix products, on_device(): jnp.einsum('cpn,isn->cips', dft_table, filtered, preferred_element_type=j...  56.9 us
    unnamed x13, local copies, waits for them, and re-layouts  40.1 us
    another operation x1, local copies, waits for them, and re-layouts, trade_parts(): got = lax.all_to_all(jnp.stack(pieces), axis, 0, 0)  36.5 us
    slice x1, local copies, waits for them, and re-layouts, gram_blocks(): real_half = split[:, :, :, 0].reshape(count_here, inputs_all, columns // 2)  32.4 us
    dot_general x2, matrix products, gram_blocks(): jnp.einsum('cik,cjk->cij', turned[:, first:last], turned[:, first:], pref...  25.1 us
    another operation x1, local copies, waits for them, and re-layouts, gram_blocks(): turned.reshape(count_here, inputs_all, columns // (2 * local_frame_count)...  23.7 us
  transfers between devices with their start and end apart: 3, of which 2 were waited for; matrix products, arithmetic and copies ran while one was open for 1% of the time, Pallas kernels for 0%

profile of v1, /device:TPU:0, one launch (start us, length us, event | category | flops | bytes accessed | tf_op | source)
XLA Modules:
  0.0 820.6 jit_solution(9698383115097426338)
XLA Ops:
  6.5 15.4 %copy.24 = bf16[4,8,256,1024]{3,2,1,0:T(8,128)(2,1)S(1)} copy(bf16[4,8,256,1024]{3,1,2,0:T(8,128)(2,1)} %bitcast.97) | data formatting | bytes 33554432
  22.1 4.9 collective-permute-start
  27.0 8.5 %negate_convert_fusion = (bf16[512,1,1024]{2,0,1:T(8,128)(2,1)S(1)}, bf16[512,1,1024]{2,0,1:T(8,128)(2,1)S(1)}) fusion(), kind=kLoop, calls=%fused_computation.86 | loop fusion | flops 8912896 | bytes 2097152 | tf_op jit(solution)/shard_map/convert.3
  35.9 12.0 %maximum_convert_fusion = f32[32,259,1024]{2,1,0:T(8,128)} fusion(bf16[32,256,1024]{2,1,0:T(8,128)(2,1)S(1)} %bitcast.96, bf16[32,3,1024]{2,1,0:T(4,128)(2,1)S(1)} %collective-permute-done), kind=kLoop, calls=%fused_computation.22 | loop fusion | flops 33947648 | bytes 50921472 | tf_op jit(solution)/shard_map/convert_element_type | solution.py:82
  47.9 56.9 %fusion.10 = f32[512,32,2,256]{0,3,2,1:T(8,128)} fusion(f32[32,259,1024]{2,1,0:T(8,128)} %maximum_convert_fusion, f32[1024]{0:T(1024)S(1)} %bitcast.100, f32[1024]{0:T(1024)S(1)} %bitcast.101, f32[1024]{0:T(1024)S(1)} %bitcast.99, f32[1024]{0:T(1024)S(1)} %bitcast.98, bf16[512,1,1024]{2,0,1:T(8,128)(2,1)S(1)} %get-tuple-element.15, ...), kind=kOutput, calls=%fused_computation.33 | convolution fusion | flops 17251172352 | bytes 169885696 | tf_op jit(solution)/shard_map/cpn,isn->cips/dot_general | solution.py:91
  104.8 12.3 %multiply_convert_fusion = (bf16[512,32,256]{0,2,1:T(8,128)(2,1)S(1)}, bf16[512,32,256]{0,2,1:T(8,128)(2,1)S(1)}) fusion(f32[512,32,2,256]{0,3,2,1:T(8,128)} %fusion.10, f32[512,32]{0,1:T(8,128)S(1)} %get-tuple-element.14, f32[512,32]{0,1:T(8,128)S(1)} %get-tuple-element.13), kind=kLoop, calls=%fused_computation.28 | loop fusion | flops 41943040 | bytes 50462720 | tf_op jit(solution)/shard_map/convert.1
  117.1 2.4 fusion.22
  119.5 3.2 fusion.25
  122.7 2.4 fusion.28
  125.0 3.2 fusion.31
  128.2 2.3 fusion.34
  130.5 3.2 fusion.37
  133.7 2.4 fusion.19
  136.1 3.2 fusion.43
  139.3 36.5 %copy.15 = bf16[8,64,32,512]{3,2,1,0:T(8,128)(2,1)} copy(bf16[8,64,32,512]{1,3,2,0:T(8,128)(2,1)} %fusion.43) | data formatting | bytes 33554432 | tf_op jit(solution)/shard_map/stack | solution.py:10
  175.8 5.7 all-to-all-start
  181.7 183.8 %all-to-all-done = bf16[8,64,32,512]{3,2,1,0:T(8,128)(2,1)} async-done(((bf16[8,64,32,512]{3,2,1,0:T(8,128)(2,1)}), bf16[8,64,32,512]{3,2,1,0:T(8,128)(2,1)}, u32[]{:S(2)}, u32[]{:S(2)}) %all-to-all-start) | async-done | bytes 16777248 | tf_op jit(solution)/shard_map/all_to_all | solution.py:10
  365.5 14.1 %copy.16 = bf16[64,8,32,512]{3,2,1,0:T(8,128)(2,1)} copy(bf16[64,8,32,512]{3,2,0,1:T(8,128)(2,1)} %bitcast.18) | data formatting | bytes 33554432 | tf_op jit(solution)/shard_map/reshape | solution.py:11
  379.6 23.7 %reshape_reshape.3 = bf16[64,256,1,2,256]{4,3,1,0,2:T(2,128)(2,1)} reshape(bf16[64,8,32,512]{3,2,1,0:T(8,128)(2,1)} %copy.16) | data formatting | bytes 33554432 | tf_op jit(solution)/shard_map/reshape;reshape | solution.py:41
  403.3 32.4 %fusion.68 = (bf16[64,256,1,1,256]{4,3,1,0,2:T(2,128)(2,1)}, bf16[64,256,1,1,256]{4,3,1,0,2:T(2,128)(2,1)}) fusion(bf16[64,256,1,2,256]{4,3,1,0,2:T(2,128)(2,1)} %reshape_reshape.3), kind=kLoop, calls=%fused_computation.100 | loop fusion | bytes 33554432 | tf_op jit(solution)/shard_map/slice | solution.py:44
  435.7 8.9 %copy.27 = bf16[64,256,1,1,256]{4,1,0,3,2:T(8,128)(2,1)S(1)} copy(bf16[64,256,1,1,256]{4,3,1,0,2:T(2,128)(2,1)} %get-tuple-element.7) | data formatting | bytes 16777216
  444.6 11.9 %copy.28 = bf16[64,256,1,1,256]{4,1,0,3,2:T(8,128)(2,1)S(1)} copy(bf16[64,256,1,1,256]{4,3,1,0,2:T(2,128)(2,1)} %get-tuple-element.8) | data formatting | bytes 16777216
  456.6 3.2 copy-done.1
  459.8 3.3 fusion.44
  463.1 9.5 %fusion.38 = f32[64,128,256]{2,1,0:T(8,128)} fusion(bf16[64,256,256]{2,1,0:T(8,128)(2,1)} %bitcast.92, bf16[64,256,256]{2,1,0:T(8,128)(2,1)S(1)} %bitcast.88), kind=kOutput, calls=%fused_computation.63 | convolution fusion | flops 1073741824 | bytes 20971520 | tf_op jit(solution)/shard_map/cik,cjk->cij/dot_general | solution.py:63
  472.6 6.8 fusion.60
  479.4 10.1 %fusion.13 = f32[64,128,128]{2,1,0:T(8,128)} fusion(bf16[64,256,512]{2,1,0:T(8,128)(2,1)} %bitcast.85), kind=kOutput, calls=%fused_computation.34 | convolution fusion | flops 1073741824 | bytes 12582912 | tf_op jit(solution)/shard_map/cik,cjk->cij/dot_general | solution.py:51
  489.5 15.0 %pad_select_fusion = f32[64,128,256]{2,1,0:T(8,128)} fusion(f32[64,128,128]{2,1,0:T(8,128)} %fusion.60, pred[128,256]{1,0:T(8,128)(4,1)S(1)} %iota_compare_fusion.1, bf16[64,256,512]{2,1,0:T(8,128)(2,1)} %bitcast.86), kind=kOutput, calls=%fused_computation.41 | convolution fusion | flops 2149580800 | bytes 37781504 | tf_op jit(solution)/shard_map/cik,cjk->cij/dot_general | solution.py:51
  504.6 14.2 %subtract_select_fusion = f32[64,128,256]{2,1,0:T(8,128)} fusion(f32[64,128,256]{2,1,0:T(8,128)} %fusion.38, f32[64,128,128]{2,1,0:T(8,128)} %fusion.13, pred[128,256]{1,0:T(8,128)(4,1)S(1)} %iota_compare_fusion, bf16[64,256,256]{2,1,0:T(8,128)(2,1)} %bitcast.90, bf16[64,256,256]{2,1,0:T(8,128)(2,1)} %bitcast.94), kind=kOutput, calls=%fused_computation.40 | convolution fusion | flops 1077936128 | bytes 33587200 | tf_op jit(solution)/shard_map/cik,cjk->cij/dot_general | solution.py:57
  518.8 11.4 %maximum_multiply_fusion = f32[64,256,256]{2,1,0:T(8,128)} fusion(f32[64,128,256]{2,1,0:T(8,128)} %subtract_select_fusion, f32[64,128,256]{2,1,0:T(8,128)} %pad_select_fusion), kind=kLoop, calls=%fused_computation.25 | loop fusion | flops 8388608 | bytes 33554432 | tf_op jit(solution)/shard_map/div | solution.py:73
  530.9 278.1 %reduce-scatter.2.cloned.1.call-done = f32[16,256,256]{2,1,0:T(8,128)} async-done(((f32[64,256,256]{2,1,0:T(8,128)}), f32[16,256,256]{2,1,0:T(8,128)}) %reduce-scatter.2.cloned.1.call-update) | async-done | bytes 4194320 | tf_op jit(solution)/shard_map/reduce_scatter | solution.py:106
  809.0 4.7 broadcast_multiply_fusion
  (20 shorter events, 1.3 us)
Async XLA Ops:
  6.5 29.0 %copy-start.3 = (f32[32]{0:T(128)S(1)}, f32[32]{0:T(128)}, u32[]{:S(2)}) copy-start(f32[32]{0:T(128)} %param.6) | copy-start | bytes 388
  6.5 29.3 %copy-start.2 = (f32[4,1024]{1,0:T(4,128)S(1)}, f32[4,1024]{1,0:T(4,128)}, u32[]{:S(2)}) copy-start(f32[4,1024]{1,0:T(4,128)} %param.5) | copy-start | bytes 49156
  22.1 13.8 %collective-permute-start = (bf16[32,3,1024]{2,1,0:T(4,128)(2,1)S(1)}, bf16[32,3,1024]{2,1,0:T(4,128)(2,1)S(1)}, u32[]{:S(2)}, u32[]{:S(2)}) collective-permute-start(bf16[32,3,1024]{2,1,0:T(4,128)(2,1)S(1)} %slice.79), channel_id=1, source_target_pairs={{0,1},{1,2},{2,3},{4,5},{5,6},{6,7},{8,9},{9,10},{10,11},{12,13},{... | collective-permute-start | bytes 589832 | tf_op jit(solution)/shard_map/ppermute | solution.py:17
  175.8 189.7 %all-to-all-start = ((bf16[8,64,32,512]{3,2,1,0:T(8,128)(2,1)}), bf16[8,64,32,512]{3,2,1,0:T(8,128)(2,1)}, u32[]{:S(2)}, u32[]{:S(2)}) async-start(bf16[8,64,32,512]{3,2,1,0:T(8,128)(2,1)} %copy.15), calls=%async_computation | async-start | bytes 33554432 | tf_op jit(solution)/shard_map/all_to_all | solution.py:10
  181.5 627.5 %reduce-scatter.2.cloned.1.call-start = ((), (), s32[]{:S(2)}) async-start(), calls=%async_computation.2 | async-start | bytes 20971520 | tf_op jit(solution)/shard_map/reduce_scatter | solution.py:106
  444.6 28.0 %copy-start = (bf16[64,256,1,1,256]{4,1,0,3,2:T(8,128)(2,1)}, bf16[64,256,1,1,256]{4,1,0,3,2:T(8,128)(2,1)S(1)}, u32[]{:S(2)}) copy-start(bf16[64,256,1,1,256]{4,1,0,3,2:T(8,128)(2,1)S(1)} %copy.27) | copy-start | bytes 25165828
  456.6 3.2 copy-start.1
  530.2 0.7 copy-start.4
Sparse Core Ops, SparseCore 0:
  530.4 278.6 reduce-scatter.1
